TPU v7x, 128 devices: a whole 4x4x4 slice. The times are simulated.
128 devices in a mesh: row: 8 (over y, z_lo), col: 16 (over z_hi, x, core).
Axes of the slice: x: 4, y: 4, z: 4 (z_hi: 2, z_lo: 2; z = z_hi * 2 + z_lo), core: 2. Of those that a mesh axis runs over, the one named last changes fastest.
Arguments:
- kernel: bfloat16 [20480, 20480], P('row', 'col'), may hold values from -2.861023e-06 to 2.861023e-06
- occ: bfloat16 [20480, 128], P(('row', 'col')), may hold values from -6 to 6
- virt: bfloat16 [20480, 512], P(('col', 'row')), may hold values from -6 to 6
- rhs: float32 [128, 512], replicated, may hold values from -6 to 6
- e_occ: float32 [128], replicated, may hold values from -2 to -0.5
- e_virt: float32 [512], replicated, may hold values from 0.2 to 3
Outputs:
- amplitudes: float32 [128, 512], replicated
All inputs are finite; a program needn't handle non-finite values.
Results may differ from a plain program's by a relative error of at most 0.0045.
Values may be sent and summed in bfloat16 or wider, within the bound.
No kernel may reach another device: no remote copies, remote signals or barrier semaphores. Data moves between devices by JAX's collectives and lax.ppermute only.
A program may use at most 64 MiB of HBM per device.

v0:
```python
import math
import jax
import jax.numpy as jnp
from jax import lax
from jax.sharding import PartitionSpec as P

ITERS = 2


def in_order(pieces, dim):
    pieces = jnp.moveaxis(pieces, 0, dim)
    dims = pieces.shape
    return pieces.reshape(*dims[:dim], dims[dim] * dims[dim + 1], *dims[dim + 2 :])


def sent_to_all(shard, axis):
    peers = lax.axis_size(axis)
    return lax.all_to_all(
        jnp.broadcast_to(shard[None], (peers, *shard.shape)), axis, 0, 0, tiled=True
    )


def gather_directly(shard, axis, dim):
    return in_order(sent_to_all(shard, axis), dim)


def body(kernel, occ, virt, rhs, e_occ, e_virt):
    denom = e_virt[None, :] - e_occ[:, None]
    amplitudes = rhs / denom
    virt_cols = gather_directly(virt, "row", 0)
    occ_full = lax.all_gather(occ, "col", axis=0, tiled=True)

    def fold(total, pieces, start):
        resp_rows, occ_piece = pieces
        kern_rows = lax.dynamic_slice_in_dim(kernel, start, resp_rows.shape[0], 0)
        outer = lax.dot_general(
            resp_rows, virt_cols, (((1,), (1,)), ((), ())), preferred_element_type=jnp.float32
        )
        weighted = (kern_rows.astype(jnp.float32) * outer).astype(jnp.bfloat16)
        return total + lax.dot_general(
            occ_piece, weighted, (((0,), (0,)), ((), ())), preferred_element_type=jnp.float32
        )

    for step in range(ITERS):
        amp_b = amplitudes.astype(jnp.bfloat16)
        empty = jnp.zeros((occ.shape[1], virt_cols.shape[0]), jnp.float32)
        resp_full = jnp.dot(occ_full, amp_b, preferred_element_type=jnp.float32).astype(
            jnp.bfloat16
        )
        height = occ_full.shape[0]
        block = math.gcd(height, 512)

        def add_block(index, total):
            start = (index * block).astype(jnp.int32)
            pieces = (
                lax.dynamic_slice_in_dim(resp_full, start, block, 0),
                lax.dynamic_slice_in_dim(occ_full, start, block, 0),
            )
            return fold(total, pieces, start)

        partial_sum = lax.fori_loop(0, height // block, add_block, empty)
        projection = jnp.dot(
            partial_sum, virt_cols.astype(jnp.float32), precision=lax.Precision.HIGHEST
        )
        exchange = lax.psum(projection, ("row", "col"))
        amplitudes = (rhs - exchange) / denom
    return amplitudes


def solution(mesh):
    in_specs = (P("row", "col"), P(("row", "col"), None), P(("col", "row"), None), P(), P(), P())
    out_specs = P()
    return jax.shard_map(body, mesh=mesh, in_specs=in_specs, out_specs=out_specs, check_vma=False)
```

profile of v0, /device:TPU:1, one launch (start us, length us, event | category | flops | bytes accessed | tf_op | source)
XLA Modules:
  0.0 371.0 jit_solution(7374602793152194372)
XLA Ops:
  6.5 0.0 copy-start.1
  6.5 0.0 copy-start
  6.5 0.0 copy-start.3
  6.5 0.0 copy-start.2
  6.5 2.1 broadcast_in_dim.2
  8.7 6.4 %all-to-all-start = ((bf16[8,160,512]{2,1,0:T(8,128)(2,1)}), bf16[8,160,512]{2,1,0:T(8,128)(2,1)S(1)}, u32[]{:S(2)}, u32[]{:S(2)}) async-start(bf16[8,160,512]{2,1,0:T(8,128)(2,1)} %broadcast_in_dim.2), calls=%async_computation | async-start | bytes 2621440 | tf_op jit(solution)/shard_map/all_to_all | solution.py:18
  15.0 0.0 all-reduce.3.cloned.1.call-start
  15.1 0.0 copy-done.1
  15.1 28.9 %all_gather.3 = bf16[2560,128]{1,0:T(8,128)(2,1)S(1)} all-gather(bf16[160,128]{1,0:T(8,128)(2,1)S(1)} %copy-done.1), channel_id=1, replica_groups=mesh['row'=8,'col'=16] {'col'}, dimensions={0}, use_global_device_ids=true | all-gather | bytes 696320 | tf_op jit(solution)/shard_map/all_gather | solution.py:31
  44.0 0.0 copy-done
  44.0 0.0 copy-done.3
  44.0 0.0 copy-done.2
  44.0 2.4 fusion.14
  46.5 0.0 all-to-all-done
  46.5 14.5 %while.28 = (s32[]{:T(128)}, f32[128,1280]{1,0:T(8,128)S(1)}, bf16[2560,128]{1,0:T(8,128)(2,1)S(1)}, bf16[2560,1280]{1,0:T(8,128)(2,1)}, bf16[2560,512]{1,0:T(8,...) while((s32[]{:T(128)}, f32[128,1280]{1,0:T(8,128)S(1)}, ...), condition=%wide.region_1.0_spmd.clone, body=%wide.region_0.0_spmd.clone.sunk | while | flops 841154560 | bytes 4589724 | solution.py:61
  46.5 2.9 convolution_add_fusion.4
  49.4 2.9 convolution_add_fusion.4
  52.3 2.9 convolution_add_fusion.4
  55.2 2.9 convolution_add_fusion.4
  58.1 2.9 convolution_add_fusion.4
  61.0 1.4 fusion.24
  62.4 0.0 all-reduce.3.cloned.1.call-update
  62.4 0.0 all-reduce.5.cloned.1.call-start
  62.5 139.9 %all-reduce.3.cloned.1.call-done = f32[128,512]{1,0:T(8,128)} async-done(((f32[128,512]{1,0:T(8,128)}), f32[128,512]{1,0:T(8,128)}) %all-reduce.3.cloned.1.call-update) | async-done | bytes 262160 | tf_op jit(solution)/shard_map/psum | solution.py:65
  202.4 3.4 fusion.15
  205.8 14.5 %while.29 = (s32[]{:T(128)}, f32[128,1280]{1,0:T(8,128)S(1)}, bf16[2560,128]{1,0:T(8,128)(2,1)S(1)}, bf16[2560,1280]{1,0:T(8,128)(2,1)}, bf16[2560,512]{1,0:T(8,...) while((s32[]{:T(128)}, f32[128,1280]{1,0:T(8,128)S(1)}, ...), condition=%wide.region_4.0_spmd.clone, body=%wide.region_3.0_spmd.clone.sunk | while | flops 841154560 | bytes 4589724 | solution.py:61
  205.8 2.9 convolution_add_fusion.5
  208.7 2.9 convolution_add_fusion.5
  211.6 2.9 convolution_add_fusion.5
  214.5 2.9 convolution_add_fusion.5
  217.4 2.9 convolution_add_fusion.5
  220.3 1.4 fusion.25
  221.7 0.0 all-reduce.5.cloned.1.call-update
  221.7 140.7 %all-reduce.5.cloned.1.call-done = f32[128,512]{1,0:T(8,128)} async-done(((f32[128,512]{1,0:T(8,128)}), f32[128,512]{1,0:T(8,128)}) %all-reduce.5.cloned.1.call-update) | async-done | bytes 262160 | tf_op jit(solution)/shard_map/psum | solution.py:65
  362.4 1.8 subtract_divide_fusion
  (2 shorter events, 0.0 us)
Async XLA Ops:
  6.5 8.6 %copy-start.1 = (bf16[160,128]{1,0:T(8,128)(2,1)S(1)}, bf16[160,128]{1,0:T(8,128)(2,1)}, u32[]{:S(2)}) copy-start(bf16[160,128]{1,0:T(8,128)(2,1)} %param.11) | copy-start | bytes 122884
  6.5 37.5 %copy-start = (f32[128,512]{1,0:T(8,128)S(1)}, f32[128,512]{1,0:T(8,128)}, u32[]{:S(2)}) copy-start(f32[128,512]{1,0:T(8,128)} %param.13) | copy-start | bytes 786436
  6.5 37.5 %copy-start.3 = (f32[128]{0:T(128)S(1)}, f32[128]{0:T(128)}, u32[]{:S(2)}) copy-start(f32[128]{0:T(128)} %param.14) | copy-start | bytes 1540
  6.5 37.5 %copy-start.2 = (f32[512]{0:T(512)S(1)}, f32[512]{0:T(512)}, u32[]{:S(2)}) copy-start(f32[512]{0:T(512)} %param.15) | copy-start | bytes 6148
  8.7 37.8 %all-to-all-start = ((bf16[8,160,512]{2,1,0:T(8,128)(2,1)}), bf16[8,160,512]{2,1,0:T(8,128)(2,1)S(1)}, u32[]{:S(2)}, u32[]{:S(2)}) async-start(bf16[8,160,512]{2,1,0:T(8,128)(2,1)} %broadcast_in_dim.2), calls=%async_computation | async-start | bytes 2621440 | tf_op jit(solution)/shard_map/all_to_all | solution.py:18
  15.0 187.4 %all-reduce.3.cloned.1.call-start = ((), (), s32[]{:S(2)}) async-start(), calls=%async_computation.1 | async-start | bytes 524288 | tf_op jit(solution)/shard_map/psum | solution.py:65
  62.4 300.0 %all-reduce.5.cloned.1.call-start = ((), (), s32[]{:S(2)}) async-start(), calls=%async_computation.2 | async-start | bytes 524288 | tf_op jit(solution)/shard_map/psum | solution.py:65
Sparse Core Ops, SparseCore 0:
  62.5 139.8 all-reduce.2
  221.9 140.5 all-reduce.4
where the time goes:
time: 372 us; the launch traced here: 371 us
  waiting for transfers between devices  281 us (76%)
  matrix products  37.4 us (10%)
  blocking collectives  28.9 us (8%)
  between operations  13.5 us (4%)
  starting transfers between devices  6.44 us (2%)
    psum x2, waiting for transfers between devices, body(): exchange = lax.psum(projection, ('row', 'col'))  281 us
    all_gather x1, blocking collectives, body(): occ_full = lax.all_gather(occ, 'col', axis=0, tiled=True)  28.9 us
    dot_general x10, matrix products, fold(): lax.dot_general(occ_piece, weighted, (((0,), (0,)), ((), ())), preferred_...  28.8 us
  transfers between devices with their start and end apart: 3, of which 2 were waited for; matrix products, arithmetic and copies ran while one was open for 1% of the time, Pallas kernels for 0%

commit v1 on v0

--- a/solution.py
+++ b/solution.py
@@ -5,6 +5,12 @@
 from jax.sharding import PartitionSpec as P
 
 ITERS = 2
+
+
+def summed_here(array, axis):
+    terms = lax.all_gather(array, axis, axis=0, tiled=False)
+    total = terms.sum(axis=0)
+    return total
 
 
 def in_order(pieces, dim):
@@ -62,7 +68,7 @@
         projection = jnp.dot(
             partial_sum, virt_cols.astype(jnp.float32), precision=lax.Precision.HIGHEST
         )
-        exchange = lax.psum(projection, ("row", "col"))
+        exchange = summed_here(projection, ("row", "col"))
         amplitudes = (rhs - exchange) / denom
     return amplitudes
 

time: 372 us -> 575 us (1.55)
  waiting for transfers between devices: 281 us -> 462 us
  other arithmetic: 1.76 us -> 24.8 us
    all_gather x0 -> x2, waiting for transfers between devices: none -> 462 us  [summed_here(): terms = lax.all_gather(array, axis, axis=0, tiled=False)]
    psum x2 -> x0, waiting for transfers between devices: 281 us -> none  [body(): exchange = lax.psum(projection, ('row', 'col'))]
    reduce_sum x0 -> x2, other arithmetic: none -> 24 us  [summed_here(): total = terms.sum(axis=0)]
  transfers between devices with their start and end apart: 3 -> 3, of which waited for: 2 -> 2; matrix products, arithmetic and copies ran while one was open for 1% -> 0% of each run, Pallas kernels for 0% -> 0%
where the time goes in v1:
time: 575 us
  waiting for transfers between devices  462 us (80%)
  matrix products  36.5 us (6%)
  blocking collectives  28.9 us (5%)
  other arithmetic  24.8 us (4%)
  between operations  13.5 us (2%)
  starting transfers between devices  6.44 us (1%)
    all_gather x2, waiting for transfers between devices, summed_here(): terms = lax.all_gather(array, axis, axis=0, tiled=False)  462 us
    all_gather x1, blocking collectives, body(): occ_full = lax.all_gather(occ, 'col', axis=0, tiled=True)  28.9 us
    dot_general x10, matrix products, fold(): lax.dot_general(occ_piece, weighted, (((0,), (0,)), ((), ())), preferred_...  28.8 us
    reduce_sum x2, other arithmetic, summed_here(): total = terms.sum(axis=0)  24 us
  transfers between devices with their start and end apart: 3, of which 2 were waited for; matrix products, arithmetic and copies ran while one was open for 0% of the time, Pallas kernels for 0%

profile of v1, /device:TPU:1, one launch (start us, length us, event | category | flops | bytes accessed | tf_op | source)
XLA Modules:
  0.0 574.9 jit_solution(15960842556876951890)
XLA Ops:
  6.5 0.0 copy-start.1
  6.5 0.0 copy-start
  6.5 0.0 copy-start.3
  6.5 0.0 copy-start.2
  6.5 2.1 broadcast_in_dim.2
  8.7 6.4 %all-to-all-start = ((bf16[8,160,512]{2,1,0:T(8,128)(2,1)}), bf16[8,160,512]{2,1,0:T(8,128)(2,1)S(1)}, u32[]{:S(2)}, u32[]{:S(2)}) async-start(bf16[8,160,512]{2,1,0:T(8,128)(2,1)} %broadcast_in_dim.2), calls=%async_computation | async-start | bytes 2621440 | tf_op jit(solution)/shard_map/all_to_all | solution.py:24
  15.0 0.0 all-gather.5.cloned.1.call-start
  15.1 0.0 copy-done.1
  15.1 28.9 %all_gather.15 = bf16[2560,128]{1,0:T(8,128)(2,1)S(1)} all-gather(bf16[160,128]{1,0:T(8,128)(2,1)S(1)} %copy-done.1), channel_id=1, replica_groups=mesh['row'=8,'col'=16] {'col'}, dimensions={0}, use_global_device_ids=true | all-gather | bytes 696320 | tf_op jit(solution)/shard_map/all_gather | solution.py:37
  44.0 0.0 copy-done
  44.0 0.0 copy-done.3
  44.0 0.0 copy-done.2
  44.0 2.4 fusion.14
  46.5 0.0 all-to-all-done
  46.5 14.5 %while.28 = (s32[]{:T(128)}, f32[128,1280]{1,0:T(8,128)S(1)}, bf16[2560,128]{1,0:T(8,128)(2,1)S(1)}, bf16[2560,1280]{1,0:T(8,128)(2,1)}, bf16[2560,512]{1,0:T(8,...) while((s32[]{:T(128)}, f32[128,1280]{1,0:T(8,128)S(1)}, ...), condition=%wide.region_1.0_spmd.clone, body=%wide.region_0.0_spmd.clone.sunk | while | flops 841154560 | bytes 4589724 | solution.py:67
  46.5 2.9 convolution_add_fusion.4
  49.4 2.9 convolution_add_fusion.4
  52.3 2.9 convolution_add_fusion.4
  55.2 2.9 convolution_add_fusion.4
  58.1 2.9 convolution_add_fusion.4
  61.0 1.4 fusion.24
  62.4 0.0 all-gather.5.cloned.1.call-update
  62.4 0.0 all-gather.7.cloned.1.call-start
  62.5 230.2 %all-gather.5.cloned.1.call-done = f32[16384,512]{1,0:T(8,128)} async-done(((f32[128,512]{1,0:T(8,128)}), f32[16384,512]{1,0:T(8,128)}) %all-gather.5.cloned.1.call-update) | async-done | bytes 33554448 | tf_op jit(solution)/shard_map/all_gather | solution.py:11
  292.7 12.0 %reduce_sum.18 = f32[128,512]{1,0:T(8,128)S(1)} reduce(f32[128,128,512]{2,1,0:T(8,128)} %bitcast.19, f32[]{:T(128)} %constant.60.clone.1), dimensions={0}, to_apply=%region_2.0 | reduce | flops 8323072 | bytes 33816580 | tf_op jit(solution)/shard_map/reduce_sum | solution.py:12
  304.7 2.4 fusion.15
  307.1 14.5 %while.29 = (s32[]{:T(128)}, f32[128,1280]{1,0:T(8,128)S(1)}, bf16[2560,128]{1,0:T(8,128)(2,1)S(1)}, bf16[2560,1280]{1,0:T(8,128)(2,1)}, bf16[2560,512]{1,0:T(8,...) while((s32[]{:T(128)}, f32[128,1280]{1,0:T(8,128)S(1)}, ...), condition=%wide.region_4.0_spmd.clone, body=%wide.region_3.0_spmd.clone.sunk | while | flops 841154560 | bytes 4589724 | solution.py:67
  307.1 2.9 convolution_add_fusion.5
  310.0 2.9 convolution_add_fusion.5
  312.9 2.9 convolution_add_fusion.5
  315.8 2.9 convolution_add_fusion.5
  318.7 2.9 convolution_add_fusion.5
  321.6 1.4 fusion.25
  323.0 0.0 all-gather.7.cloned.1.call-update
  323.1 232.2 %all-gather.7.cloned.1.call-done = f32[16384,512]{1,0:T(8,128)} async-done(((f32[128,512]{1,0:T(8,128)}), f32[16384,512]{1,0:T(8,128)}) %all-gather.7.cloned.1.call-update) | async-done | bytes 33554448 | tf_op jit(solution)/shard_map/all_gather | solution.py:11
  555.2 12.0 %reduce_sum.19 = f32[128,512]{1,0:T(8,128)S(1)} reduce(f32[128,128,512]{2,1,0:T(8,128)} %bitcast.20, f32[]{:T(128)} %constant.60.clone.1), dimensions={0}, to_apply=%region_5.0 | reduce | flops 8323072 | bytes 33816580 | tf_op jit(solution)/shard_map/reduce_sum | solution.py:12
  567.2 0.8 subtract_divide_fusion
  (2 shorter events, 0.0 us)
Async XLA Ops:
  6.5 8.6 %copy-start.1 = (bf16[160,128]{1,0:T(8,128)(2,1)S(1)}, bf16[160,128]{1,0:T(8,128)(2,1)}, u32[]{:S(2)}) copy-start(bf16[160,128]{1,0:T(8,128)(2,1)} %param.11) | copy-start | bytes 122884
  6.5 37.5 %copy-start = (f32[128,512]{1,0:T(8,128)S(1)}, f32[128,512]{1,0:T(8,128)}, u32[]{:S(2)}) copy-start(f32[128,512]{1,0:T(8,128)} %param.13) | copy-start | bytes 786436
  6.5 37.5 %copy-start.3 = (f32[128]{0:T(128)S(1)}, f32[128]{0:T(128)}, u32[]{:S(2)}) copy-start(f32[128]{0:T(128)} %param.14) | copy-start | bytes 1540
  6.5 37.5 %copy-start.2 = (f32[512]{0:T(512)S(1)}, f32[512]{0:T(512)}, u32[]{:S(2)}) copy-start(f32[512]{0:T(512)} %param.15) | copy-start | bytes 6148
  8.7 37.8 %all-to-all-start = ((bf16[8,160,512]{2,1,0:T(8,128)(2,1)}), bf16[8,160,512]{2,1,0:T(8,128)(2,1)S(1)}, u32[]{:S(2)}, u32[]{:S(2)}) async-start(bf16[8,160,512]{2,1,0:T(8,128)(2,1)} %broadcast_in_dim.2), calls=%async_computation | async-start | bytes 2621440 | tf_op jit(solution)/shard_map/all_to_all | solution.py:24
  15.0 277.6 %all-gather.5.cloned.1.call-start = ((), (), s32[]{:S(2)}) async-start(), calls=%async_computation.1 | async-start | bytes 33816576 | tf_op jit(solution)/shard_map/all_gather | solution.py:11
  62.4 492.8 %all-gather.7.cloned.1.call-start = ((), (), s32[]{:S(2)}) async-start(), calls=%async_computation.2 | async-start | bytes 33816576 | tf_op jit(solution)/shard_map/all_gather | solution.py:11
Sparse Core Ops, SparseCore 0:
  62.5 230.0 all-gather.4
  323.2 232.0 all-gather.6
